TPU v7x, 32 devices: a whole 2x2x4 slice. The times are simulated.
32 devices in a mesh: dp: 16 (over z, x, core), tensor: 2 (over y).
Axes of the slice: x: 2, y: 2, z: 4, core: 2. Of those that a mesh axis runs over, the one named last changes fastest.
Arguments:
- tokens: bfloat16 [24576, 768], P(('dp', 'tensor')), may hold values from -6 to 6
- token_mask: int32 [1536, 16], P('dp'), may hold values from 0 to 1, as said below
- norm_gains: float32 [2, 768], replicated, may hold values from 0.5 to 1.5
- gain_moments: float32 [2, 768], replicated, may hold values from 76.8 to 614.4
- cotangent: bfloat16 [1536, 768], P(('dp', 'tensor')), may hold values from -6 to 6
- master: float32 [768, 96, 96], P(('dp', 'tensor'))
- stat_left: float32 [768, 96, 96], P(('dp', 'tensor')), as said below
- stat_right: float32 [768, 96, 96], P(('dp', 'tensor')), as said below
- root_left: float32 [768, 96, 96], P(('dp', 'tensor')), as said below
- root_right: float32 [768, 96, 96], P(('dp', 'tensor')), as said below
Outputs:
- pooled: float32 [1536, 768], P(('dp', 'tensor'))
- input_grad: float32 [24576, 768], P(('dp', 'tensor'))
- gain_grads: float32 [2, 768], replicated
- gain_moments_new: float32 [2, 768], replicated
- norm_gains_new: float32 [2, 768], replicated
- grad_blocks: float32 [768, 96, 96], P(('dp', 'tensor'))
- left_new: float32 [768, 96, 96], P(('dp', 'tensor'))
- right_new: float32 [768, 96, 96], P(('dp', 'tensor'))
- master_new: float32 [768, 96, 96], P(('dp', 'tensor'))
- master_copy: bfloat16 [768, 96, 96], P(('dp', 'tensor'))
Inputs may be any that keep to these rules, and one draw needn't show every extreme that they name: `token_mask`: each caption's mask is 1 on its first n slots and 0 after, n from 4 to 16; the first caption has n = 4 and the last n = 16. `stat_left`: each block is symmetric positive definite. `stat_right`: each block is symmetric positive definite. `root_left`: each block is symmetric positive definite. `root_right`: each block is symmetric positive definite.
All inputs are finite; a program needn't handle non-finite values.
Results may differ from a plain program's by a relative error of at most 0.0097.
Values may be sent and summed in bfloat16 or wider, within the bound.
No kernel may reach another device: no remote copies, remote signals or barrier semaphores. Data moves between devices by JAX's collectives and lax.ppermute only.
A program may use at most 192 MiB of HBM per device.

v0:
```python
import jax
import jax.numpy as jnp
from jax import lax
from jax.sharding import PartitionSpec as P

D = 768
HEADS = 12
HD = 64
FF = 3072
BLOCK = 96


EPSILON = 1e-06
DECAY_RATE = 0.5
STEP_RATE = 0.25
GAIN_RATE = 0.3
MASKED_SCORE = -1e30
PRECISE = lax.Precision.HIGHEST


def layer_norm(values, gain):
    center = values - jnp.mean(values, axis=-1, keepdims=True)
    spread = jnp.mean(center * center, axis=-1, keepdims=True)
    return center * lax.rsqrt(spread + EPSILON) * gain


def contract(left_op, right_op, left_dim, right_dim):
    return lax.dot_general(
        left_op,
        right_op,
        (((left_dim,), (right_dim,)), ((), ())),
        preferred_element_type=jnp.float32,
    )


def to_blocks(matrix):
    num_rows, num_cols = matrix.shape
    return (
        matrix.reshape(num_rows // BLOCK, BLOCK, num_cols // BLOCK, BLOCK)
        .transpose(0, 2, 1, 3)
        .reshape(-1, BLOCK, BLOCK)
    )


def unpack(blocks, shapes):
    matrices = []
    offset = 0
    for num_rows, num_cols in shapes:
        num_blocks = num_rows // BLOCK * (num_cols // BLOCK)
        chosen = blocks[offset : offset + num_blocks]
        matrices.append(
            chosen.reshape(num_rows // BLOCK, num_cols // BLOCK, BLOCK, BLOCK)
            .transpose(0, 2, 1, 3)
            .reshape(num_rows, num_cols)
        )
        offset += num_blocks
    return matrices


def attention_scores(queries, key_rows, mask_keys):
    scores = jnp.einsum(
        "cqhe,ckhe->chqk", queries, key_rows, preferred_element_type=jnp.float32
    ) * HD ** (-0.5)
    return jnp.where(mask_keys, scores, MASKED_SCORE)


def body(
    tokens,
    token_mask,
    norm_gains,
    gain_moments,
    cotangent,
    master,
    stat_left,
    stat_right,
    root_left,
    root_right,
):
    tensor_size = lax.axis_size("tensor")
    tensor_pos = lax.axis_index("tensor")
    own_rows = tokens.shape[0]
    own_caps = cotangent.shape[0]
    cap_slots = own_rows // own_caps
    local_heads = HEADS // tensor_size
    shapes = (
        (D, 3 * D // tensor_size),
        (D // tensor_size, D),
        (D, FF // tensor_size),
        (FF // tensor_size, D),
    )
    whole_blocks = lax.all_gather(master.astype(jnp.bfloat16), "dp", axis=0, tiled=True)
    w_qkv, w_out, w_up, w_down = unpack(whole_blocks, shapes)
    group_mask = token_mask.astype(jnp.float32)
    own_mask = lax.dynamic_slice_in_dim(group_mask, tensor_pos * own_caps, own_caps, 0)
    inputs = tokens.astype(jnp.float32)
    normed, norm_pull = jax.vjp(layer_norm, inputs, norm_gains[0])
    gathered = lax.all_gather(normed.astype(jnp.bfloat16), "tensor", axis=0, tiled=True)
    group_rows = gathered.shape[0]
    group_caps = group_rows // cap_slots
    mixed_qkv = jnp.dot(gathered, w_qkv, preferred_element_type=jnp.float32).astype(jnp.bfloat16)
    mixed_qkv = mixed_qkv.reshape(group_caps, cap_slots, 3, local_heads, HD)
    queries = mixed_qkv[:, :, 0]
    key_rows = mixed_qkv[:, :, 1]
    value_rows = mixed_qkv[:, :, 2]
    mask_keys = group_mask[:, None, None, :] > 0
    scores = attention_scores(queries, key_rows, mask_keys)
    top_score = jnp.max(scores, axis=-1, keepdims=True)
    exp_scores = jnp.exp(scores - top_score)
    exp_totals = jnp.sum(exp_scores, axis=-1, keepdims=True)
    log_total = top_score + jnp.log(exp_totals)
    weights = (exp_scores / exp_totals).astype(jnp.bfloat16)
    attended = jnp.einsum(
        "chqk,ckhe->cqhe", weights, value_rows, preferred_element_type=jnp.float32
    )
    attended = attended.astype(jnp.bfloat16).reshape(group_rows, local_heads * HD)
    after_attn = inputs + lax.psum_scatter(
        jnp.dot(attended, w_out, preferred_element_type=jnp.float32),
        "tensor",
        scatter_dimension=0,
        tiled=True,
    )
    normed_two, norm_two_pull = jax.vjp(layer_norm, after_attn, norm_gains[1])
    gathered_two = lax.all_gather(normed_two.astype(jnp.bfloat16), "tensor", axis=0, tiled=True)
    up_proj = jnp.dot(gathered_two, w_up, preferred_element_type=jnp.float32)
    hidden, gelu_pull = jax.vjp(jax.nn.gelu, up_proj)
    hidden_low = hidden.astype(jnp.bfloat16)
    block_out = after_attn + lax.psum_scatter(
        jnp.dot(hidden_low, w_down, preferred_element_type=jnp.float32).astype(jnp.bfloat16),
        "tensor",
        scatter_dimension=0,
        tiled=True,
    ).astype(jnp.float32)
    true_counts = jnp.sum(own_mask, axis=1)[:, None]
    pooled = (
        jnp.sum(block_out.reshape(own_caps, cap_slots, D) * own_mask[:, :, None], axis=1)
        / true_counts
    )
    cotan = cotangent.astype(jnp.float32)
    grad_out = (cotan[:, None, :] * own_mask[:, :, None] / true_counts[:, :, None]).reshape(
        own_rows, D
    )
    grad_out_all = lax.all_gather(grad_out.astype(jnp.bfloat16), "tensor", axis=0, tiled=True)
    grad_hidden = contract(grad_out_all, w_down, 1, 1)
    grad_down = contract(hidden_low, grad_out_all, 0, 0)
    grad_up_low = gelu_pull(grad_hidden)[0].astype(jnp.bfloat16)
    grad_up = contract(gathered_two, grad_up_low, 0, 0)
    grad_normed_two = lax.psum_scatter(
        contract(grad_up_low, w_up, 1, 1), "tensor", scatter_dimension=0, tiled=True
    )
    grad_after_part, gain_two_grad = norm_two_pull(grad_normed_two)
    grad_after = grad_out + grad_after_part
    grad_after_all = lax.all_gather(grad_after.astype(jnp.bfloat16), "tensor", axis=0, tiled=True)
    grad_out_proj = contract(attended, grad_after_all, 0, 0)
    grad_attended = (
        contract(grad_after_all, w_out, 1, 1)
        .astype(jnp.bfloat16)
        .reshape(group_caps, cap_slots, local_heads, HD)
    )
    scores_again = attention_scores(queries, key_rows, mask_keys)
    probs = jnp.exp(scores_again - log_total)
    grad_probs = jnp.einsum(
        "cqhe,ckhe->chqk", grad_attended, value_rows, preferred_element_type=jnp.float32
    )
    inner_sum = jnp.sum(probs * grad_probs, axis=-1, keepdims=True)
    grad_scores = (probs * (grad_probs - inner_sum)).astype(jnp.bfloat16)
    scale_factor = HD ** (-0.5)
    grad_queries = (
        jnp.einsum("chqk,ckhe->cqhe", grad_scores, key_rows, preferred_element_type=jnp.float32)
        * scale_factor
    )
    grad_keys = (
        jnp.einsum("chqk,cqhe->ckhe", grad_scores, queries, preferred_element_type=jnp.float32)
        * scale_factor
    )
    grad_values = jnp.einsum(
        "chqk,cqhe->ckhe",
        probs.astype(jnp.bfloat16),
        grad_attended,
        preferred_element_type=jnp.float32,
    )
    grad_mixed = (
        jnp.stack([grad_queries, grad_keys, grad_values], axis=2)
        .astype(jnp.bfloat16)
        .reshape(group_rows, 3 * local_heads * HD)
    )
    grad_qkv = contract(gathered, grad_mixed, 0, 0)
    grad_normed = lax.psum_scatter(
        contract(grad_mixed, w_qkv, 1, 1), "tensor", scatter_dimension=0, tiled=True
    )
    input_part, gain_one_grad = norm_pull(grad_normed)
    input_grad = grad_after + input_part
    gain_grads = lax.psum(jnp.stack([gain_one_grad, gain_two_grad], axis=0), ("dp", "tensor"))
    moments_new = DECAY_RATE * gain_moments + (1.0 - DECAY_RATE) * gain_grads * gain_grads
    gains_new = norm_gains - GAIN_RATE * gain_grads / (jnp.sqrt(moments_new) + 1e-08)
    flat_grads = jnp.concatenate(
        [to_blocks(grad_qkv), to_blocks(grad_out_proj), to_blocks(grad_up), to_blocks(grad_down)],
        axis=0,
    )
    grad_blocks = lax.psum_scatter(flat_grads, "dp", scatter_dimension=0, tiled=True)
    left_new = DECAY_RATE * stat_left + (1.0 - DECAY_RATE) * jnp.einsum(
        "nij,nkj->nik", grad_blocks, grad_blocks, precision=PRECISE
    )
    right_new = DECAY_RATE * stat_right + (1.0 - DECAY_RATE) * jnp.einsum(
        "nji,njk->nik", grad_blocks, grad_blocks, precision=PRECISE
    )
    right_side = jnp.einsum("nij,njk->nik", grad_blocks, root_right, precision=PRECISE)
    direction = jnp.einsum("nij,njk->nik", root_left, right_side, precision=PRECISE)
    master_new = master - STEP_RATE * direction
    return (
        pooled,
        input_grad,
        gain_grads,
        moments_new,
        gains_new,
        grad_blocks,
        left_new,
        right_new,
        master_new,
        master_new.astype(jnp.bfloat16),
    )


def solution(mesh):
    placed = (
        P(("dp", "tensor"), None),
        P("dp", None),
        P(),
        P(),
        P(("dp", "tensor"), None),
        P(("dp", "tensor"), None, None),
        P(("dp", "tensor"), None, None),
        P(("dp", "tensor"), None, None),
        P(("dp", "tensor"), None, None),
        P(("dp", "tensor"), None, None),
    )
    return jax.shard_map(
        body,
        mesh=mesh,
        in_specs=placed,
        out_specs=(
            P(("dp", "tensor"), None),
            P(("dp", "tensor"), None),
            P(),
            P(),
            P(),
            P(("dp", "tensor"), None, None),
            P(("dp", "tensor"), None, None),
            P(("dp", "tensor"), None, None),
            P(("dp", "tensor"), None, None),
            P(("dp", "tensor"), None, None),
        ),
        check_vma=False,
    )
```

profile of v0, /device:TPU:0, one launch (start us, length us, event | category | flops | bytes accessed | tf_op | source)
XLA Modules:
  0.0 853.8 jit_solution(11640377347928995673)
XLA Ops:
  7.3 2.3 convert_element_type.76
  12.8 82.3 %all-gather.8.cloned.1.call-done = bf16[384,96,96]{2,1,0:T(8,128)(2,1)} async-done(((bf16[24,96,96]{2,1,0:T(8,128)(2,1)}), bf16[384,96,96]{2,1,0:T(8,128)(2,1)}) %all-gather.8.cloned.1.call-update) | async-done | bytes 7077904 | tf_op jit(solution)/shard_map/all_gather | solution.py:91
  99.7 2.8 copy.117
  102.5 3.8 reshape.170
  106.4 25.0 %all-gather.6.cloned.1.call-done = bf16[1536,768]{1,0:T(8,128)(2,1)} async-done(((bf16[768,768]{1,0:T(8,128)(2,1)}), bf16[1536,768]{1,0:T(8,128)(2,1)}) %all-gather.6.cloned.1.call-update) | async-done | bytes 2359312 | tf_op jit(solution)/shard_map/all_gather | solution.py:97
  131.4 6.7 convolution_convert_fusion
  138.2 11.5 %reshape.171 = bf16[96,16,3,6,64]{4,3,2,1,0:T(8,128)(2,1)} reshape(bf16[1536,1152]{1,0:T(8,128)(2,1)} %convolution_convert_fusion) | data formatting | bytes 7077888 | tf_op jit(solution)/shard_map/reshape | solution.py:101
  149.7 4.7 fusion.45
  161.2 2.8 copy.123
  163.9 4.3 reshape.172
  168.2 3.5 fusion.48
  172.0 59.9 %reduce-scatter.6.cloned.1.call-done = f32[768,768]{1,0:T(8,128)} async-done(((f32[1536,768]{1,0:T(8,128)}), f32[768,768]{1,0:T(8,128)}) %reduce-scatter.6.cloned.1.call-update) | async-done | bytes 2359312 | tf_op jit(solution)/shard_map/reduce_scatter | solution.py:116
  231.9 2.3 fusion.43
  248.5 5.6 fusion.44
  254.1 2.8 copy.182
  256.9 6.4 reshape.176
  263.3 4.8 copy.181
  268.2 6.0 reshape.178
  274.1 10.3 %fusion.49 = f32[1536,1536]{1,0:T(8,128)} fusion(bf16[1536,768]{1,0:T(8,128)(2,1)} %all-gather.10.cloned.1.call-done, bf16[768,1536]{1,0:T(8,128)(2,1)} %reshape.176), kind=kOutput, calls=%fused_computation.104 | convolution fusion | flops 3623878656 | bytes 14155776 | tf_op jit(solution)/shard_map/dot_general | solution.py:124
  284.4 26.6 %all-gather.12.cloned.1.call-done = bf16[1536,768]{1,0:T(8,128)(2,1)} async-done(((bf16[768,768]{1,0:T(8,128)(2,1)}), bf16[1536,768]{1,0:T(8,128)(2,1)}) %all-gather.12.cloned.1.call-update) | async-done | bytes 2359312 | tf_op jit(solution)/shard_map/all_gather | solution.py:142
  311.0 12.2 %fusion.6 = bf16[1536,1536]{1,0:T(8,128)(2,1)S(1)} fusion(f32[1536,1536]{1,0:T(8,128)} %fusion.49, bf16[1536,768]{1,0:T(8,128)(2,1)} %all-gather.12.cloned.1.call-done, bf16[1536,768]{1,0:T(8,128)(2,1)} %reshape.178), kind=kOutput, calls=%fused_computation.9 | convolution fusion | flops 3671064576 | bytes 18874368 | tf_op jit(solution)/shard_map/dot_general | solution.py:28
  325.4 5.4 fusion.50
  330.9 10.3 %convolution_convert_fusion.1 = bf16[1536,768]{1,0:T(8,128)(2,1)} fusion(bf16[1536,768]{1,0:T(8,128)(2,1)} %reshape.178, f32[1536,1536]{1,0:T(8,128)} %fusion.49), kind=kOutput, calls=%fused_computation.30 | convolution fusion | flops 3646291968 | bytes 14155776 | tf_op jit(solution)/shard_map/dot_general | solution.py:128
  341.2 49.8 %reduce-scatter.10.cloned.1.call-done = f32[768,768]{1,0:T(8,128)} async-done(((f32[1536,768]{1,0:T(8,128)}), f32[768,768]{1,0:T(8,128)}) %reduce-scatter.10.cloned.1.call-update) | async-done | bytes 2359312 | tf_op jit(solution)/shard_map/reduce_scatter | solution.py:147
  391.0 3.0 multiply_reduce_fusion.1
  394.6 33.9 %reduce-scatter.8.cloned.1.call-done = bf16[768,768]{1,0:T(8,128)(2,1)} async-done(((bf16[1536,768]{1,0:T(8,128)(2,1)}), bf16[768,768]{1,0:T(8,128)(2,1)}) %reduce-scatter.8.cloned.1.call-update) | async-done | bytes 1179664 | tf_op jit(solution)/shard_map/reduce_scatter | solution.py:127
  428.6 4.4 fusion.41
  436.1 36.1 %all-gather.14.cloned.1.call-done = bf16[1536,768]{1,0:T(8,128)(2,1)} async-done(((bf16[768,768]{1,0:T(8,128)(2,1)}), bf16[1536,768]{1,0:T(8,128)(2,1)}) %all-gather.14.cloned.1.call-update) | async-done | bytes 2359312 | tf_op jit(solution)/shard_map/all_gather | solution.py:152
  472.2 4.1 convolution_convert_fusion.2
  476.3 4.8 reshape.180
  481.1 6.3 multiply_reduce_fusion
  487.5 2.8 fusion.19
  492.2 3.6 fusion.26
  495.8 2.7 fusion.27
  498.5 3.2 copy.134
  501.7 5.9 copy.132
  507.6 5.9 copy.131
  513.5 3.8 multiply_bitcast_fusion
  517.4 2.7 maximum_convert_fusion
  520.1 15.9 %copy.136 = bf16[96,16,3,6,64]{4,3,2,1,0:T(8,128)(2,1)} copy(bf16[96,16,3,6,64]{0,4,3,2,1:T(8,128)(2,1)} %maximum_convert_fusion) | data formatting | bytes 7077888 | tf_op jit(solution)/shard_map/convert_element_type | solution.py:183
  536.0 12.0 %convert_element_type.94 = bf16[1536,1152]{1,0:T(8,128)(2,1)} reshape(bf16[96,16,3,6,64]{4,3,2,1,0:T(8,128)(2,1)} %copy.136) | data formatting | bytes 7077888 | tf_op jit(solution)/shard_map/convert_element_type | solution.py:183
  548.0 7.4 fusion.51
  555.5 4.4 copy.137
  561.4 12.0 %fusion.39 = f32[1536,768]{1,0:T(8,128)} fusion(bf16[1536,768]{1,0:T(8,128)(2,1)} %all-gather.12.cloned.1.call-done, f32[1536,1536]{1,0:T(8,128)} %fusion.49), kind=kOutput, calls=%fused_computation.95 | convolution fusion | flops 3645112320 | bytes 16515072 | tf_op jit(solution)/shard_map/dot_general | solution.py:28
  573.4 7.9 reshape.187
  581.3 6.7 copy.142
  588.0 5.7 fusion.54
  593.7 7.7 reshape.185
  601.4 7.6 copy.141
  609.1 2.5 copy.140
  611.6 5.9 copy.138
  617.5 2.8 fusion.53
  620.6 3.8 fusion.52
  625.1 7.6 pad_maximum_fusion
  635.9 2.2 multiply_reduce_fusion.3
  638.9 2.4 fusion.18
  643.6 2.7 add_add_fusion.2
  646.3 42.0 %psum.7 = f32[2,768]{1,0:T(2,128)S(1)} all-reduce(f32[2,768]{1,0:T(2,128)S(1)} %pad_maximum_fusion.1), channel_id=1, replica_groups=mesh['dp'=16,'tensor'=2] {'dp','tensor'}, use_global_device_ids=true, to_apply=%region_19.20 | all-reduce | flops 1536 | bytes 12288 | tf_op jit(solution)/shard_map/psum | solution.py:192
  689.6 138.9 %reduce-scatter.14.cloned.1.call-done = f32[24,96,96]{2,1,0:T(8,128)} async-done(((f32[384,96,96]{2,1,0:T(8,128)}), f32[24,96,96]{2,1,0:T(8,128)}) %reduce-scatter.14.cloned.1.call-update) | async-done | bytes 884752 | tf_op jit(solution)/shard_map/reduce_scatter | solution.py:199
  828.5 3.3 fusion.55
  831.9 3.3 fusion.47
  835.1 2.2 copy.147
  838.7 4.4 fusion.32
  843.2 3.6 fusion.33
  (208 shorter events, 48.1 us)
Async XLA Ops:
  7.2 824.7 %copy-start = (f32[24,96,96]{2,1,0:T(8,128)S(1)}, f32[24,96,96]{2,1,0:T(8,128)}, u32[]{:S(2)}) copy-start(f32[24,96,96]{2,1,0:T(8,128)} %param.18) | copy-start | bytes 2654212
  7.2 2.5 copy-start.53
  7.2 2.5 copy-start.2
  7.2 87.9 %all-gather.8.cloned.1.call-start = ((), (), s32[]{:S(2)}) async-start(), calls=%async_computation.6 | async-start | bytes 10027008 | tf_op jit(solution)/shard_map/all_gather | solution.py:91
  9.6 121.8 %all-gather.6.cloned.1.call-start = ((), (), s32[]{:S(2)}) async-start(), calls=%async_computation.5 | async-start | bytes 3538944 | tf_op jit(solution)/shard_map/all_gather | solution.py:97
  10.5 85.8 %copy-start.46 = (f32[768]{0:T(1024)}, f32[768]{0:T(1024)S(1)}, u32[]{:S(2)}) copy-start(f32[768]{0:T(1024)S(1)} %fusion.17) | copy-start | bytes 9220
  10.5 85.8 %copy-start.42 = (f32[768]{0:T(1024)}, f32[768]{0:T(1024)S(1)}, u32[]{:S(2)}) copy-start(f32[768]{0:T(1024)S(1)} %fusion.35) | copy-start | bytes 9220
  12.0 220.0 %reduce-scatter.6.cloned.1.call-start = ((), (), s32[]{:S(2)}) async-start(), calls=%async_computation.7 | async-start | bytes 7077888 | tf_op jit(solution)/shard_map/reduce_scatter | solution.py:116
  106.4 31.8 %copy-start.30 = (bf16[768,1152]{0,1:T(8,128)(2,1)}, bf16[768,1152]{0,1:T(8,128)(2,1)S(1)}, u32[]{:S(2)}) copy-start(bf16[768,1152]{0,1:T(8,128)(2,1)S(1)} %reshape.170) | copy-start | bytes 5308420
  149.7 4.8 copy-start.56
  154.4 2.7 copy-start.14
  154.4 4.4 copy-start.11
  157.1 2.4 copy-start.1
  157.1 2.4 copy-start.32
  158.8 2.4 copy-start.34
  163.9 4.3 copy-start.21
  168.2 3.5 copy-start.9
  171.8 102.3 %all-gather.10.cloned.1.call-start = ((), (), s32[]{:S(2)}) async-start(), calls=%async_computation.8 | async-start | bytes 3538944 | tf_op jit(solution)/shard_map/all_gather | solution.py:123
  236.6 74.4 %all-gather.12.cloned.1.call-start = ((), (), s32[]{:S(2)}) async-start(), calls=%async_computation.10 | async-start | bytes 3538944 | tf_op jit(solution)/shard_map/all_gather | solution.py:142
  248.5 142.5 %reduce-scatter.10.cloned.1.call-start = ((), (), s32[]{:S(2)}) async-start(), calls=%async_computation.11 | async-start | bytes 7077888 | tf_op jit(solution)/shard_map/reduce_scatter | solution.py:147
  311.0 14.4 %copy-start.26 = (bf16[768,1536]{1,0:T(8,128)(2,1)S(1)}, bf16[768,1536]{1,0:T(8,128)(2,1)}, u32[]{:S(2)}) copy-start(bf16[768,1536]{1,0:T(8,128)(2,1)} %reshape.176) | copy-start | bytes 7077892
  330.8 97.7 %reduce-scatter.8.cloned.1.call-start = ((), (), s32[]{:S(2)}) async-start(), calls=%async_computation.9 | async-start | bytes 3538944 | tf_op jit(solution)/shard_map/reduce_scatter | solution.py:127
  341.2 131.0 %all-gather.14.cloned.1.call-start = ((), (), s32[]{:S(2)}) async-start(), calls=%async_computation.12 | async-start | bytes 3538944 | tf_op jit(solution)/shard_map/all_gather | solution.py:152
  391.0 3.0 copy-start.49
  428.6 5.9 copy-start.28
  428.6 5.9 copy-start.44
  433.0 3.0 copy-start.50
  434.4 37.8 %copy-start.22 = (bf16[384,768]{1,0:T(8,128)(2,1)S(1)}, bf16[384,768]{1,0:T(8,128)(2,1)}, u32[]{:S(2)}) copy-start(bf16[384,768]{1,0:T(8,128)(2,1)} %reshape.174) | copy-start | bytes 1769476
  436.0 202.9 %reduce-scatter.12.cloned.1.call-start = ((), (), s32[]{:S(2)}) async-start(), calls=%async_computation.13 | async-start | bytes 7077888 | tf_op jit(solution)/shard_map/reduce_scatter | solution.py:187
  476.3 11.2 %slice-start = ((s8[4718592]{0:T(1024)(128)(4,1)}), s8[524288]{0:T(1024)(128)(4,1)S(1)}, s32[]{:S(2)}) async-start(s8[4718592]{0:T(1024)(128)(4,1)} %bitcast.136), calls=%async_computation.15 | async-start | bytes 1048576
  481.1 6.4 slice-start.1
  481.1 6.4 copy-start.8
  492.2 3.6 copy-start.13
  495.8 2.7 copy-start.16
  513.5 3.8 copy-start.17
  536.0 12.0 %copy-start.31 = (bf16[768,1152]{0,1:T(8,128)(2,1)S(1)}, bf16[768,1152]{0,1:T(8,128)(2,1)}, u32[]{:S(2)}) copy-start(bf16[768,1152]{0,1:T(8,128)(2,1)} %copy-done.30) | copy-start | bytes 5308420
  555.5 273.1 %reduce-scatter.14.cloned.1.call-start = ((), (), s32[]{:S(2)}) async-start(), calls=%async_computation.14 | async-start | bytes 20054016 | tf_op jit(solution)/shard_map/reduce_scatter | solution.py:199
  555.5 4.4 copy-start.10
  573.4 14.6 %slice-start.7 = ((s8[4718592]{0:T(1024)(128)(4,1)}), s8[524288]{0:T(1024)(128)(4,1)S(1)}, s32[]{:S(2)}) async-start(s8[4718592]{0:T(1024)(128)(4,1)} %bitcast.166), calls=%async_computation.22 | async-start | bytes 1048576
  581.3 6.7 copy-start.59
  581.3 6.7 slice-start.8
  601.4 7.6 copy-start.23
  611.6 6.0 copy-start.25
  617.5 2.9 copy-start.20
  617.5 3.1 copy-start.24
  620.3 4.1 slice-start.2
  620.3 4.1 slice-start.4
  620.6 3.9 slice-start.3
  620.6 4.5 slice-start.5
  633.9 5.0 copy-start.3
  633.9 5.0 copy-start.39
  633.9 5.0 copy-start.41
  635.3 2.8 copy-start.58
  638.1 3.2 copy-start.47
  638.1 3.3 copy-start.43
  638.9 2.5 copy-start.5
  641.4 2.2 copy-start.7
  641.4 2.2 copy-start.29
  643.6 2.7 copy-start.57
  643.6 184.9 %copy-start.36 = (f32[24,96,96]{2,1,0:T(8,128)S(1)}, f32[24,96,96]{2,1,0:T(8,128)}, u32[]{:S(2)}) copy-start(f32[24,96,96]{2,1,0:T(8,128)} %param.19) | copy-start | bytes 2654212
  646.3 185.6 %copy-start.19 = (f32[24,96,96]{1,2,0:T(8,128)S(1)}, f32[24,96,96]{1,2,0:T(8,128)}, u32[]{:S(2)}) copy-start(f32[24,96,96]{1,2,0:T(8,128)} %copy.145) | copy-start | bytes 2654212
  688.2 146.9 %copy-start.54 = (f32[2,768]{1,0:T(2,128)}, f32[2,768]{1,0:T(2,128)S(1)}, u32[]{:S(2)}) copy-start(f32[2,768]{1,0:T(2,128)S(1)} %psum.7) | copy-start | bytes 18436
  835.1 3.6 copy-start.4
  838.7 4.4 copy-start.37
  (16 other events, 24.2 us)
Sparse Core Ops, SparseCore 0:
  10.9 84.1 all-gather.7
  97.2 34.1 all-gather.5
  171.9 59.9 reduce-scatter.5
  236.7 36.0 all-gather.9
  274.9 36.0 all-gather.11
  331.0 59.9 reduce-scatter.9
  393.8 34.7 reduce-scatter.7
  436.1 36.0 all-gather.13
  555.6 59.9 reduce-scatter.11
  632.8 195.6 reduce-scatter.13
where the time goes:
time: 859 us; the launch traced here: 854 us
  waiting for transfers between devices  453 us (53%)
  local copies, waits for them, and re-layouts  173 us (20%)
  matrix products  118 us (14%)
  other arithmetic  52.3 us (6%)
  blocking collectives  42 us (5%)
  between operations  15.1 us (2%)
    reduce_scatter x1, waiting for transfers between devices, body(): lax.psum_scatter(flat_grads, 'dp', scatter_dimension=0, tiled=True)  139 us
    all_gather x1, waiting for transfers between devices, body(): lax.all_gather(master.astype(jnp.bfloat16), 'dp', axis=0, tiled=True)  82.3 us
    reduce_scatter x1, waiting for transfers between devices, body(): lax.psum_scatter(jnp.dot(attended, w_out, preferred_element_type=jnp.floa...  59.9 us
    dot_general x8, matrix products, contract(): lax.dot_general(left_op, right_op, (((left_dim,), (right_dim,)), ((), ())...  53.5 us
    reduce_scatter x1, waiting for transfers between devices, body(): lax.psum_scatter(contract(grad_up_low, w_up, 1, 1), 'tensor', scatter_dim...  49.8 us
    psum x1, blocking collectives, body(): lax.psum(jnp.stack([gain_one_grad, gain_two_grad], axis=0), ('dp', 'tenso...  42 us
    all_gather x1, waiting for transfers between devices, body(): lax.all_gather(grad_after.astype(jnp.bfloat16), 'tensor', axis=0, tiled=T...  36.1 us
    reduce_scatter x1, waiting for transfers between devices, body(): lax.psum_scatter(jnp.dot(hidden_low, w_down, preferred_element_type=jnp.f...  33.9 us
  transfers between devices with their start and end apart: 10, of which 8 were waited for; matrix products, arithmetic and copies ran while one was open for 19% of the time, Pallas kernels for 0%

commit v1 on v0

v1 whole, which is shorter than its diff:
```python
import functools

import jax
import jax.numpy as jnp
from jax import lax
from jax.experimental import pallas as pl
from jax.experimental.pallas import tpu as pltpu
from jax.sharding import PartitionSpec as P

D = 768
HEADS = 12
HD = 64
FF = 3072
BLOCK = 96
SLOTS = 16
HALVES = 2
STRIP = 4 * BLOCK
STRIPS = 96
GROUP = 128
PAIR = 2 * HD

EPSILON = 1e-06
DECAY_RATE = 0.5
STEP_RATE = 0.25
GAIN_RATE = 0.3
MASKED_SCORE = -1e30
PRECISE = lax.Precision.HIGHEST
F32 = jnp.float32
BF16 = jnp.bfloat16
VMEM_BYTES = 56 << 20


def mm(left, right, left_dim=1, right_dim=0):
    return lax.dot_general(
        left, right, (((left_dim,), (right_dim,)), ((), ())), preferred_element_type=F32
    )


def flat(block):
    return block.reshape(-1, block.shape[-1])


def norm_parts(values):
    center = values - jnp.mean(values, axis=-1, keepdims=True)
    inverse = lax.rsqrt(jnp.mean(center * center, axis=-1, keepdims=True) + EPSILON)
    return center * inverse, inverse


def norm_back(xhat, inverse, gain, grad):
    scaled = grad * gain
    return inverse * (
        scaled
        - jnp.mean(scaled, axis=-1, keepdims=True)
        - xhat * jnp.mean(scaled * xhat, axis=-1, keepdims=True)
    )


def score_bias(mask_row):
    rows = lax.broadcasted_iota(jnp.int32, (GROUP, GROUP), 0) // SLOTS
    cols = lax.broadcasted_iota(jnp.int32, (GROUP, GROUP), 1) // SLOTS
    seen = (rows == cols) & (jnp.broadcast_to(mask_row, (GROUP, GROUP)) > 0)
    bias = jnp.where(seen, 0.0, MASKED_SCORE)
    return jnp.concatenate([bias, bias], axis=0)


def split_pair(values):
    first = lax.broadcasted_iota(jnp.int32, (GROUP, PAIR), 1) < HD
    zero = jnp.zeros_like(values)
    return jnp.concatenate(
        [jnp.where(first, values, zero), jnp.where(first, zero, values)], axis=0
    )


def join_pair(stacked):
    first = lax.broadcasted_iota(jnp.int32, (GROUP, PAIR), 1) < HD
    return jnp.where(first, stacked[:GROUP], stacked[GROUP:])


def pair_probs(queries, key_rows, bias):
    scores = mm(split_pair(queries), key_rows, 1, 1) * HD ** (-0.5) + bias
    shifted = jnp.exp(scores - jnp.max(scores, axis=-1, keepdims=True))
    return shifted / jnp.sum(shifted, axis=-1, keepdims=True)


def attention_forward(
    tok, gains, mask, w_qkv, w_out, normed, qkv, attended, after, normed_two, total
):
    half = pl.program_id(0)
    rows = tok.shape[0]

    @pl.when(half == 0)
    def _():
        @pl.loop(0, rows // GROUP)
        def _(i):
            span = pl.ds(pl.multiple_of(i * GROUP, GROUP), GROUP)
            xhat, _ = norm_parts(tok[span, :].astype(F32))
            normed[span, :] = (xhat * gains[0:1, :]).astype(BF16)

    for part in range(3):
        qkv[part] = mm(normed[...], flat(w_qkv[0, :, part])).astype(BF16)

    @pl.loop(0, rows // GROUP)
    def _(i):
        span = pl.ds(pl.multiple_of(i * GROUP, GROUP), GROUP)
        bias = score_bias(mask[i])
        for pair in range(STRIP // PAIR):
            lanes = slice(pair * PAIR, (pair + 1) * PAIR)
            probs = pair_probs(qkv[0, span, lanes], qkv[1, span, lanes], bias)
            mixed = mm(probs.astype(BF16), qkv[2, span, lanes])
            attended[0, span, lanes] = join_pair(mixed).astype(BF16)

    for part in range(2):
        lanes = slice(part * STRIP, (part + 1) * STRIP)
        partial = mm(attended[0], flat(w_out[0, :, part]))

        @pl.when(half == 0)
        def _():
            total[:, lanes] = partial

        @pl.when(half > 0)
        def _():
            total[:, lanes] += partial

    @pl.when(half == HALVES - 1)
    def _():
        @pl.loop(0, rows // GROUP)
        def _(i):
            span = pl.ds(pl.multiple_of(i * GROUP, GROUP), GROUP)
            summed = tok[span, :].astype(F32) + total[span, :]
            after[span, :] = summed
            xhat, _ = norm_parts(summed)
            normed_two[span, :] = (xhat * gains[1:2, :]).astype(BF16)


GELU_A = 0.7978845608028654
GELU_B = 0.044715


def gelu_both(v):
    square = v * v
    inner = jnp.tanh(GELU_A * v * (1.0 + GELU_B * square))
    half_up = 0.5 * (1.0 + inner)
    slope = half_up + (0.5 * GELU_A) * v * (1.0 - inner * inner) * (1.0 + (3.0 * GELU_B) * square)
    return v * half_up, slope


def spread(cot, share):
    captions = cot.shape[0]
    return (
        jnp.broadcast_to(cot[:, None, :], (captions, SLOTS, cot.shape[-1])).reshape(
            captions * SLOTS, cot.shape[-1]
        )
        * share
    )


def mlp_both(
    normed_two,
    after,
    cot,
    share,
    w_up,
    w_down,
    pooled,
    grad_normed_two,
    grad_up_w,
    grad_down_w,
    out_low,
    hidden,
    grad_up,
    total,
):
    step = pl.program_id(0)
    rows = normed_two.shape[0]
    chunk = 256

    @pl.when(step == 0)
    def _():
        total[...] = after[...]
        grad_normed_two[...] = jnp.zeros_like(grad_normed_two)

        @pl.loop(0, rows // GROUP)
        def _(i):
            span = pl.ds(pl.multiple_of(i * GROUP, GROUP), GROUP)
            caps = pl.ds(pl.multiple_of(i * (GROUP // SLOTS), GROUP // SLOTS), GROUP // SLOTS)
            out_low[span, :] = spread(cot[caps, :], share[span, :]).astype(BF16)

    @pl.loop(0, rows // chunk)
    def _(i):
        span = pl.ds(pl.multiple_of(i * chunk, chunk), chunk)
        up = mm(normed_two[span, :], flat(w_up[0, :, 0]))
        grad_hidden = mm(out_low[span, 0:STRIP], flat(w_down[0, :, 0]), 1, 1)
        grad_hidden += mm(out_low[span, STRIP:], flat(w_down[0, :, 1]), 1, 1)
        act, slope = gelu_both(up)
        act = act.astype(BF16)
        grad = (grad_hidden * slope).astype(BF16)
        hidden[span, :] = act
        grad_up[span, :] = grad
        for part in range(2):
            lanes = slice(part * STRIP, (part + 1) * STRIP)
            total[span, lanes] += mm(act, flat(w_down[0, :, part]))
        grad_normed_two[span, :] += mm(grad, flat(w_up[0, :, 0]), 1, 1)

    for part in range(2):
        lanes = slice(part * STRIP, (part + 1) * STRIP)
        grad_w = mm(hidden[...], out_low[:, lanes], 0, 0)
        grad_down_w[0, :, part] = grad_w.astype(BF16).reshape(4, BLOCK, STRIP)
    grad_w = mm(normed_two[...], grad_up[...], 0, 0)
    grad_up_w[0, :, 0] = grad_w.astype(BF16).reshape(8, BLOCK, STRIP)

    @pl.when(step == pl.num_programs(0) - 1)
    def _():
        @pl.loop(0, rows // GROUP)
        def _(i):
            span = pl.ds(pl.multiple_of(i * GROUP, GROUP), GROUP)
            caps = pl.ds(pl.multiple_of(i * (GROUP // SLOTS), GROUP // SLOTS), GROUP // SLOTS)
            weighted = (total[span, :] * share[span, :]).reshape(GROUP // SLOTS, SLOTS, D)
            pooled[caps, :] = jnp.sum(weighted, axis=1)


def attention_backward(
    tok,
    gains,
    mask,
    normed,
    qkv,
    attended,
    after,
    cot,
    share,
    grad_normed_two,
    w_qkv,
    w_out,
    input_grad,
    gain_part,
    grad_qkv_w,
    grad_out_w,
    grad_after,
    after_low,
    grad_att,
    grad_mixed,
    grad_normed,
):
    half = pl.program_id(0)
    rows = tok.shape[0]

    @pl.when(half == 0)
    def _():
        gain_part[...] = jnp.zeros_like(gain_part)

        @pl.loop(0, rows // GROUP)
        def _(i):
            span = pl.ds(pl.multiple_of(i * GROUP, GROUP), GROUP)
            caps = pl.ds(pl.multiple_of(i * (GROUP // SLOTS), GROUP // SLOTS), GROUP // SLOTS)
            xhat, inverse = norm_parts(after[span, :])
            grad = grad_normed_two[span, :]
            gain_part[1:2, :] += jnp.sum(grad * xhat, axis=0, keepdims=True)
            value = spread(cot[caps, :], share[span, :]) + norm_back(
                xhat, inverse, gains[1:2, :], grad
            )
            grad_after[span, :] = value
            after_low[span, :] = value.astype(BF16)

    grad = mm(after_low[:, 0:STRIP], flat(w_out[0, :, 0]), 1, 1)
    grad += mm(after_low[:, STRIP:], flat(w_out[0, :, 1]), 1, 1)
    grad_att[...] = grad.astype(BF16)
    for part in range(2):
        lanes = slice(part * STRIP, (part + 1) * STRIP)
        grad_w = mm(attended[0], after_low[:, lanes], 0, 0)
        grad_out_w[0, :, part] = grad_w.astype(BF16).reshape(4, BLOCK, STRIP)

    @pl.loop(0, rows // GROUP)
    def _(i):
        span = pl.ds(pl.multiple_of(i * GROUP, GROUP), GROUP)
        bias = score_bias(mask[i])
        for pair in range(STRIP // PAIR):
            lanes = slice(pair * PAIR, (pair + 1) * PAIR)
            queries, key_rows, value_rows = (qkv[part, span, lanes] for part in range(3))
            probs = pair_probs(queries, key_rows, bias)
            grads = split_pair(grad_att[span, lanes])
            grad_probs = mm(grads, value_rows, 1, 1)
            inner = jnp.sum(probs * grad_probs, axis=-1, keepdims=True)
            grad_scores = (probs * (grad_probs - inner)).astype(BF16)
            scale = HD ** (-0.5)
            grad_mixed[0, span, lanes] = (join_pair(mm(grad_scores, key_rows)) * scale).astype(BF16)
            grad_mixed[1, span, lanes] = (
                mm(grad_scores, split_pair(queries), 0, 0) * scale
            ).astype(BF16)
            grad_mixed[2, span, lanes] = mm(probs.astype(BF16), grads, 0, 0).astype(BF16)

    for part in range(3):
        grad_w = mm(normed[...], grad_mixed[part], 0, 0)
        grad_qkv_w[0, :, part] = grad_w.astype(BF16).reshape(8, BLOCK, STRIP)
    back = mm(grad_mixed[0], flat(w_qkv[0, :, 0]), 1, 1)
    back += mm(grad_mixed[1], flat(w_qkv[0, :, 1]), 1, 1)
    back += mm(grad_mixed[2], flat(w_qkv[0, :, 2]), 1, 1)

    @pl.when(half == 0)
    def _():
        grad_normed[...] = back

    @pl.when(half > 0)
    def _():
        grad_normed[...] += back

    @pl.when(half == HALVES - 1)
    def _():
        @pl.loop(0, rows // GROUP)
        def _(i):
            span = pl.ds(pl.multiple_of(i * GROUP, GROUP), GROUP)
            xhat, inverse = norm_parts(tok[span, :].astype(F32))
            grad = grad_normed[span, :]
            gain_part[0:1, :] += jnp.sum(grad * xhat, axis=0, keepdims=True)
            input_grad[span, :] = grad_after[span, :] + norm_back(
                xhat, inverse, gains[0:1, :], grad
            )


def whole(shape):
    return pl.BlockSpec(shape, lambda i: (0,) * len(shape))


def shape_of(*shape, dtype=BF16):
    return jax.ShapeDtypeStruct(shape, dtype)


def cost(flops, bytes_accessed):
    return pl.CostEstimate(flops=flops, bytes_accessed=bytes_accessed, transcendentals=0)


PARAMS = dict(dimension_semantics=("arbitrary",), vmem_limit_bytes=VMEM_BYTES)


def run_forward(tok, gains, mask, strips):
    rows = tok.shape[0]
    by_three = strips.reshape(HALVES, 32, 3, BLOCK, STRIP)
    by_two = strips.reshape(HALVES, 48, 2, BLOCK, STRIP)
    return pl.pallas_call(
        attention_forward,
        grid=(HALVES,),
        in_specs=[
            whole((rows, D)),
            whole((2, D)),
            whole((rows // GROUP, 1, GROUP)),
            pl.BlockSpec((1, 8, 3, BLOCK, STRIP), lambda i: (i, 0, 0, 0, 0)),
            pl.BlockSpec((1, 4, 2, BLOCK, STRIP), lambda i: (i, 3, 0, 0, 0)),
        ],
        out_specs=[
            whole((rows, D)),
            pl.BlockSpec((3, rows, STRIP), lambda i: (i, 0, 0)),
            pl.BlockSpec((1, rows, STRIP), lambda i: (i, 0, 0)),
            whole((rows, D)),
            whole((rows, D)),
        ],
        out_shape=[
            shape_of(rows, D),
            shape_of(6, rows, STRIP),
            shape_of(2, rows, STRIP),
            shape_of(rows, D, dtype=F32),
            shape_of(rows, D),
        ],
        scratch_shapes=[pltpu.VMEM((rows, D), F32)],
        compiler_params=pltpu.CompilerParams(**PARAMS),
        cost_estimate=cost(4_600_000_000, 16_000_000),
        name="attention_forward",
    )(tok, gains, mask, by_three, by_two)


def run_mlp(normed_two, after, cot, share, strips):
    rows = normed_two.shape[0]
    by_four = strips.reshape(HALVES, 24, 4, BLOCK, STRIP)
    by_two = strips.reshape(HALVES, 48, 2, BLOCK, STRIP)
    return pl.pallas_call(
        mlp_both,
        grid=(8,),
        in_specs=[
            whole((rows, D)),
            whole((rows, D)),
            whole((rows // SLOTS, D)),
            whole((rows, 1)),
            pl.BlockSpec((1, 8, 1, BLOCK, STRIP), lambda i: (i // 4, 1, i % 4, 0, 0)),
            pl.BlockSpec((1, 4, 2, BLOCK, STRIP), lambda i: (i // 4, 8 + i % 4, 0, 0, 0)),
        ],
        out_specs=[
            whole((rows // SLOTS, D)),
            whole((rows, D)),
            pl.BlockSpec((1, 8, 1, BLOCK, STRIP), lambda i: (i // 4, 0, i % 4, 0, 0)),
            pl.BlockSpec((1, 4, 2, BLOCK, STRIP), lambda i: (i // 4, i % 4, 0, 0, 0)),
        ],
        out_shape=[
            shape_of(rows // SLOTS, D, dtype=F32),
            shape_of(rows, D, dtype=F32),
            shape_of(HALVES, 8, 4, BLOCK, STRIP),
            shape_of(HALVES, 16, 2, BLOCK, STRIP),
        ],
        scratch_shapes=[
            pltpu.VMEM((rows, D), BF16),
            pltpu.VMEM((rows, STRIP), BF16),
            pltpu.VMEM((rows, STRIP), BF16),
            pltpu.VMEM((rows, D), F32),
        ],
        compiler_params=pltpu.CompilerParams(**PARAMS),
        cost_estimate=cost(22_000_000_000, 30_000_000),
        name="mlp_both",
    )(normed_two, after, cot, share, by_four, by_two)


def run_backward(tok, gains, mask, normed, qkv, attended, after, cot, share, grad_two, strips):
    rows = tok.shape[0]
    by_three = strips.reshape(HALVES, 32, 3, BLOCK, STRIP)
    by_two = strips.reshape(HALVES, 48, 2, BLOCK, STRIP)
    return pl.pallas_call(
        attention_backward,
        grid=(HALVES,),
        in_specs=[
            whole((rows, D)),
            whole((2, D)),
            whole((rows // GROUP, 1, GROUP)),
            whole((rows, D)),
            pl.BlockSpec((3, rows, STRIP), lambda i: (i, 0, 0)),
            pl.BlockSpec((1, rows, STRIP), lambda i: (i, 0, 0)),
            whole((rows, D)),
            whole((rows // SLOTS, D)),
            whole((rows, 1)),
            whole((rows, D)),
            pl.BlockSpec((1, 8, 3, BLOCK, STRIP), lambda i: (i, 0, 0, 0, 0)),
            pl.BlockSpec((1, 4, 2, BLOCK, STRIP), lambda i: (i, 3, 0, 0, 0)),
        ],
        out_specs=[
            whole((rows, D)),
            whole((2, D)),
            pl.BlockSpec((1, 8, 3, BLOCK, STRIP), lambda i: (i, 0, 0, 0, 0)),
            pl.BlockSpec((1, 4, 2, BLOCK, STRIP), lambda i: (i, 0, 0, 0, 0)),
        ],
        out_shape=[
            shape_of(rows, D, dtype=F32),
            shape_of(2, D, dtype=F32),
            shape_of(HALVES, 8, 3, BLOCK, STRIP),
            shape_of(HALVES, 4, 2, BLOCK, STRIP),
        ],
        scratch_shapes=[
            pltpu.VMEM((rows, D), F32),
            pltpu.VMEM((rows, D), BF16),
            pltpu.VMEM((rows, STRIP), BF16),
            pltpu.VMEM((3, rows, STRIP), BF16),
            pltpu.VMEM((rows, D), F32),
        ],
        compiler_params=pltpu.CompilerParams(**PARAMS),
        cost_estimate=cost(12_000_000_000, 25_000_000),
        name="attention_backward",
    )(tok, gains, mask, normed, qkv, attended, after, cot, share, grad_two, by_three, by_two)


def to_strips(blocks):
    count = blocks.shape[0] // 4
    return blocks.reshape(count, 4, BLOCK, BLOCK).transpose(0, 2, 1, 3).reshape(count, BLOCK, STRIP)


def to_blocks(strips):
    count = strips.shape[0]
    return strips.reshape(count, BLOCK, 4, BLOCK).transpose(0, 2, 1, 3).reshape(-1, BLOCK, BLOCK)


EVERY = ("tensor", "dp")


def gather_weights(master):
    low = master.astype(BF16)
    own = low.shape[0]
    if own % 4 == 0:
        strips = to_strips(low).reshape(-1, STRIP)
        strips = lax.all_gather(strips, EVERY, axis=0, tiled=True)
        return strips.reshape(HALVES, STRIPS, BLOCK, STRIP)
    blocks = lax.all_gather(low, EVERY, axis=0, tiled=True)
    return to_strips(blocks).reshape(HALVES, STRIPS, BLOCK, STRIP)


def scatter_grads(strips, own):
    if own % 4 == 0:
        mine = lax.psum_scatter(
            strips.reshape(-1, STRIP), EVERY, scatter_dimension=0, tiled=True
        )
        return to_blocks(mine.reshape(-1, BLOCK, STRIP)).astype(F32)
    blocks = to_blocks(strips.reshape(-1, BLOCK, STRIP))
    return lax.psum_scatter(blocks, EVERY, scatter_dimension=0, tiled=True).astype(F32)


def body(
    tokens,
    token_mask,
    norm_gains,
    gain_moments,
    cotangent,
    master,
    stat_left,
    stat_right,
    root_left,
    root_right,
):
    rows = tokens.shape[0]
    own_caps = cotangent.shape[0]
    strips = gather_weights(master)
    group_mask = token_mask.astype(F32)
    own_mask = lax.dynamic_slice_in_dim(
        group_mask, lax.axis_index("tensor") * own_caps, own_caps, 0
    )
    share = (own_mask / jnp.sum(own_mask, axis=1, keepdims=True)).reshape(rows, 1)
    mask = own_mask.reshape(rows // GROUP, 1, GROUP)
    cot = cotangent.astype(F32)
    normed, qkv, attended, after, normed_two = run_forward(tokens, norm_gains, mask, strips)
    pooled, grad_two, grad_up_w, grad_down_w = run_mlp(normed_two, after, cot, share, strips)
    input_grad, gain_part, grad_qkv_w, grad_out_w = run_backward(
        tokens, norm_gains, mask, normed, qkv, attended, after, cot, share, grad_two, strips
    )
    all_grads = jnp.concatenate(
        [
            part.reshape(HALVES, -1, BLOCK, STRIP)
            for part in (grad_qkv_w, grad_out_w, grad_up_w, grad_down_w)
        ],
        axis=1,
    )
    grad_blocks = scatter_grads(all_grads, master.shape[0])
    gain_grads = lax.psum(gain_part, ("dp", "tensor"))
    moments_new = DECAY_RATE * gain_moments + (1.0 - DECAY_RATE) * gain_grads * gain_grads
    gains_new = norm_gains - GAIN_RATE * gain_grads / (jnp.sqrt(moments_new) + 1e-08)
    left_new = DECAY_RATE * stat_left + (1.0 - DECAY_RATE) * jnp.einsum(
        "nij,nkj->nik", grad_blocks, grad_blocks, precision=PRECISE
    )
    right_new = DECAY_RATE * stat_right + (1.0 - DECAY_RATE) * jnp.einsum(
        "nji,njk->nik", grad_blocks, grad_blocks, precision=PRECISE
    )
    right_side = jnp.einsum("nij,njk->nik", grad_blocks, root_right, precision=PRECISE)
    direction = jnp.einsum("nij,njk->nik", root_left, right_side, precision=PRECISE)
    master_new = master - STEP_RATE * direction
    return (
        pooled,
        input_grad,
        gain_grads,
        moments_new,
        gains_new,
        grad_blocks,
        left_new,
        right_new,
        master_new,
        master_new.astype(BF16),
    )


def solution(mesh):
    rows = P(("dp", "tensor"), None)
    blocks = P(("dp", "tensor"), None, None)
    return jax.shard_map(
        body,
        mesh=mesh,
        in_specs=(rows, P("dp", None), P(), P(), rows) + (blocks,) * 5,
        out_specs=(rows, rows, P(), P(), P()) + (blocks,) * 5,
        check_vma=False,
    )
```

time: 859 us -> 422 us (0.49)
  waiting for transfers between devices: 453 us -> 224 us
  local copies, waits for them, and re-layouts: 173 us -> 11.4 us
  matrix products: 118 us -> 7.52 us
  Pallas kernels: 0 us -> 110 us
  other arithmetic: 52.3 us -> 15.6 us
    reduce_scatter x5 -> x1, waiting for transfers between devices: 283 us -> 119 us  [scatter_grads(): lax.psum_scatter(strips.reshape(-1, STRIP), EVERY, scatter_dimension=0, t...]
    pallas_call x0 -> x3, Pallas kernels: none -> 110 us  [the longest x1 43.6 us: run_mlp(): pl.pallas_call(mlp_both, grid=(8,), in_specs=[whole((rows, D)), whole((ro...]
    dot_general x18 -> x0, matrix products: 103 us -> none  [the longest x8 53.5 us: contract(): lax.dot_general(left_op, right_op, (((left_dim,), (right_dim,)), ((), ())...]
    all_gather x5 -> x1, waiting for transfers between devices: 170 us -> 105 us  [gather_weights(): strips = lax.all_gather(strips, EVERY, axis=0, tiled=True)]
    reshape x15 -> x2, local copies, waits for them, and re-layouts: 65.3 us -> 1.65 us  [the longest x1 0.98 us: body(): (own_mask / jnp.sum(own_mask, axis=1, keepdims=True)).reshape(rows, 1)]
    convert_element_type x3 -> x0, local copies, waits for them, and re-layouts: 30.7 us -> none  [the longest x2 27.9 us: body(): grad_mixed = jnp.stack([grad_queries, grad_keys, grad_values], axis=2).as...]
    dot_general x7 -> x0, local copies, waits for them, and re-layouts: 29.3 us -> none  [the longest x4 14.3 us: contract(): lax.dot_general(left_op, right_op, (((left_dim,), (right_dim,)), ((), ())...]
    reduce_sum x11 -> x1, other arithmetic: 20.2 us -> 0.09 us  [body(): jnp.sum(own_mask, axis=1, keepdims=True)]
  transfers between devices with their start and end apart: 10 -> 2, of which waited for: 8 -> 2; matrix products, arithmetic and copies ran while one was open for 19% -> 1% of each run, Pallas kernels for 0% -> 0%
where the time goes in v1:
time: 422 us; the launch traced here: 421 us
  waiting for transfers between devices  224 us (53%)
  Pallas kernels  110 us (26%)
  blocking collectives  38.7 us (9%)
  other arithmetic  15.6 us (4%)
  between operations  14.2 us (3%)
  local copies, waits for them, and re-layouts  11.4 us (3%)
  matrix products  7.52 us (2%)
    reduce_scatter x1, waiting for transfers between devices, scatter_grads(): lax.psum_scatter(strips.reshape(-1, STRIP), EVERY, scatter_dimension=0, t...  119 us
    all_gather x1, waiting for transfers between devices, gather_weights(): strips = lax.all_gather(strips, EVERY, axis=0, tiled=True)  105 us
    pallas_call x1, Pallas kernels, run_mlp(): pl.pallas_call(mlp_both, grid=(8,), in_specs=[whole((rows, D)), whole((ro...  43.6 us
    pallas_call x1, Pallas kernels, run_backward(): pl.pallas_call(attention_backward, grid=(HALVES,), in_specs=[whole((rows,...  42.3 us
    psum x1, blocking collectives, body(): gain_grads = lax.psum(gain_part, ('dp', 'tensor'))  38.7 us
    pallas_call x1, Pallas kernels, run_forward(): pl.pallas_call(attention_forward, grid=(HALVES,), in_specs=[whole((rows,...  24.3 us
    concatenate x1, other arithmetic, body(): jnp.concatenate([part.reshape(HALVES, -1, BLOCK, STRIP) for part in (grad...  10.9 us
  transfers between devices with their start and end apart: 2, of which 2 were waited for; matrix products, arithmetic and copies ran while one was open for 1% of the time, Pallas kernels for 0%

profile of v1, /device:TPU:0, one launch (start us, length us, event | category | flops | bytes accessed | tf_op | source)
XLA Modules:
  0.0 421.5 jit_solution(16610087114994337502)
XLA Ops:
  7.2 0.0 copy-start
  7.2 0.0 all-gather.2.cloned.1.call-start
  7.2 1.4 convert_element_type.16
  8.7 0.0 copy-start.8
  8.7 0.3 copy.39
  9.0 0.0 copy-start.5
  9.0 1.2 reshape_reshape.18
  10.2 0.0 all-gather.2.cloned.1.call-update
  10.2 0.0 reduce-scatter.2.cloned.1.call-start
  10.3 0.0 copy-done.8
  10.3 0.1 fusion.6
  10.4 0.1 copy.38
  10.4 0.7 reshape.57.mask
  11.1 0.1 copy.41
  11.2 1.0 reshape.58.share
  12.2 0.0 copy-done.5
  12.2 0.7 convert_element_type.17.cot
  12.9 104.5 %all-gather.2.cloned.1.call-done = bf16[18432,384]{1,0:T(8,128)(2,1)} async-done(((bf16[576,384]{1,0:T(8,128)(2,1)}), bf16[18432,384]{1,0:T(8,128)(2,1)}) %all-gather.2.cloned.1.call-update) | async-done | bytes 14155792 | tf_op jit(solution)/shard_map/all_gather | solution.py:472
  117.4 24.3 %attention_forward.1 = (bf16[768,768]{1,0:T(8,128)(2,1)}, bf16[6,768,384]{2,1,0:T(8,128)(2,1)}, bf16[2,768,384]{2,1,0:T(8,128)(2,1)}, f32[768,768]{1,0:T(8,128)}, bf16[768,768]{1,0:T(8,128)(2,1)}) custom-call(bf16[768,768]{1,0:T(8,128)(2,1)} %tok.3, f32[2,768]{1,0:T(2,128)} %gains.3, f32[6,1,128]{2,1,0:T(1,128)} %reshape.57.mask, ...), custom_call_target="tpu_custom_call" | custom-call | flops 4600000000 | bytes 16000000 | tf_op jit(solution)/shard_map/attention_forward/pallas_call | solution.py:338
  141.7 43.6 %mlp_both.1 = (f32[48,768]{1,0:T(8,128)}, f32[768,768]{1,0:T(8,128)}, bf16[2,8,4,96,384]{4,3,2,1,0:T(8,128)(2,1)}, bf16[2,16,2,96,384]{4,3,2,1,0:T(8,128)(2,1)}) custom-call(bf16[768,768]{1,0:T(8,128)(2,1)} %get-tuple-element.23.normed_two, f32[768,768]{1,0:T(8,128)} %get-tuple-element.24.after, f32[48,768]{1,0:T(8,128)} %convert_element_type.17.cot, ...), custom_call_target="tpu_custom_call" | custom-call | flops 22000001024 | bytes 30000000 | tf_op jit(solution)/shard_map/mlp_both/pallas_call | solution.py:373
  185.3 0.0 slice-start
  185.4 0.0 slice-start.1
  185.4 42.3 %attention_backward.1 = (f32[768,768]{1,0:T(8,128)}, f32[2,768]{1,0:T(2,128)}, bf16[2,8,3,96,384]{4,3,2,1,0:T(8,128)(2,1)}, bf16[2,4,2,96,384]{4,3,2,1,0:T(8,128)(2,1)}) custom-call(bf16[768,768]{1,0:T(8,128)(2,1)} %tok.3, f32[2,768]{1,0:T(2,128)} %gains.3, f32[6,1,128]{2,1,0:T(1,128)} %reshape.57.mask, bf16[768,768]{1,0:T(8,128)(2,1)} %get-tuple-element.26.normed, ...), custom_call_target="tpu_custom_call" | custom-call | flops 12000000000 | bytes 25000000 | tf_op jit(solution)/shard_map/attention_backward/pallas_call | solution.py:412
  227.7 0.0 slice-done
  227.7 0.0 slice-done.1
  227.7 10.9 %pad_maximum_fusion = bf16[2,96,96,384]{3,2,1,0:T(8,128)(2,1)} fusion(bf16[2,32,96,384]{3,2,1,0:T(8,128)(2,1)} %bitcast.41, bf16[2,32,96,384]{3,2,1,0:T(8,128)(2,1)S(1)} %bitcast.40, bf16[2,8,96,384]{3,2,1,0:T(8,128)(2,1)} %bitcast.45, bf16[2,24,96,384]{3,2,1,0:T(8,128)(2,1)} %bitcast.42), kind=kLoop, calls=%fused_computation | loop fusion | flops 21233664 | bytes 28311552 | tf_op jit(solution)/shard_map/concatenate | solution.py:515
  238.6 0.0 copy-start.1
  238.6 0.0 reduce-scatter.2.cloned.1.call-update
  238.6 1.2 copy-done.1
  239.9 0.0 copy-start.9
  239.9 0.0 copy-start.6
  239.9 0.4 copy.48
  240.2 0.3 copy-done.9
  240.6 38.7 %psum.7 = f32[2,768]{1,0:T(2,128)S(1)} all-reduce(f32[2,768]{1,0:T(2,128)S(1)} %copy-done.9), channel_id=1, replica_groups=mesh['dp'=16,'tensor'=2] {'dp','tensor'}, use_global_device_ids=true, to_apply=%region_1.0 | all-reduce | flops 1536 | bytes 12288 | tf_op jit(solution)/shard_map/psum | solution.py:523
  279.2 0.0 copy-done.6
  279.2 0.0 copy-start.7
  279.2 1.3 divide_subtract_fusion
  280.6 119.2 %reduce-scatter.2.cloned.1.call-done = bf16[576,384]{1,0:T(8,128)(2,1)} async-done(((bf16[18432,384]{1,0:T(8,128)(2,1)}), bf16[576,384]{1,0:T(8,128)(2,1)}) %reduce-scatter.2.cloned.1.call-update) | async-done | bytes 442384 | tf_op jit(solution)/shard_map/reduce_scatter | solution.py:480
  399.7 1.4 reshape_reshape.22
  401.2 0.1 copy.45
  401.3 0.0 copy-start.4
  401.3 1.2 bitcast_convert_fusion
  402.5 0.0 copy-done.7
  402.5 0.5 copy-done.4
  402.9 1.1 fusion.8
  404.1 0.0 copy-done
  404.1 3.5 fusion.7
  407.5 2.7 copy.49
  410.2 0.0 copy-start.2
  410.2 1.0 copy.50
  411.2 0.4 copy-done.2
  411.7 0.0 copy-start.3
  411.7 1.4 fusion.2
  413.1 0.0 copy-done.3
  413.1 1.5 fusion.3
  (2 shorter events, 0.0 us)
Async XLA Ops:
  7.2 396.9 %copy-start = (f32[24,96,96]{2,1,0:T(8,128)S(1)}, f32[24,96,96]{2,1,0:T(8,128)}, u32[]{:S(2)}) copy-start(f32[24,96,96]{2,1,0:T(8,128)} %param.18) | copy-start | bytes 2654212
  7.2 110.2 %all-gather.2.cloned.1.call-start = ((), (), s32[]{:S(2)}) async-start(), calls=%async_computation.1 | async-start | bytes 14598144 | tf_op jit(solution)/shard_map/all_gather | solution.py:472
  8.7 1.6 copy-start.8
  9.0 3.2 copy-start.5
  10.2 389.5 %reduce-scatter.2.cloned.1.call-start = ((), (), s32[]{:S(2)}) async-start(), calls=%async_computation.2 | async-start | bytes 14598144 | tf_op jit(solution)/shard_map/reduce_scatter | solution.py:480
  185.3 42.4 %slice-start = ((s8[4718592]{0:T(1024)(128)(4,1)}), s8[4194304]{0:T(1024)(128)(4,1)S(1)}, s32[]{:S(2)}) async-start(s8[4718592]{0:T(1024)(128)(4,1)} %bitcast.38), calls=%async_computation.3 | async-start | bytes 8388608
  185.4 42.4 %slice-start.1 = ((s8[4718592]{0:T(1024)(128)(4,1)}), s8[524288]{0:T(1024)(128)(4,1)S(1)}, s32[]{:S(2)}) async-start(s8[4718592]{0:T(1024)(128)(4,1)} %bitcast.38), calls=%async_computation.4 | async-start | bytes 1048576
  238.6 1.3 copy-start.1
  239.9 0.7 copy-start.9
  239.9 39.4 %copy-start.6 = (f32[2,768]{1,0:T(2,128)S(1)}, f32[2,768]{1,0:T(2,128)}, u32[]{:S(2)}) copy-start(f32[2,768]{1,0:T(2,128)} %gains.3) | copy-start | bytes 18436
  279.2 123.2 %copy-start.7 = (f32[2,768]{1,0:T(2,128)}, f32[2,768]{1,0:T(2,128)S(1)}, u32[]{:S(2)}) copy-start(f32[2,768]{1,0:T(2,128)S(1)} %psum.7) | copy-start | bytes 18436
  401.3 1.7 copy-start.4
  410.2 1.5 copy-start.2
  411.7 1.4 copy-start.3
Sparse Core Ops, SparseCore 0:
  11.5 105.8 all-gather.1
  238.7 160.9 reduce-scatter.1
